TPU v7x, 512 devices: a whole 4x8x8 slice. The times are simulated.
512 devices in a mesh: subj: 32 (over z, y_lo), slab: 16 (over y_hi, x, core).
Axes of the slice: x: 4, y: 8 (y_hi: 2, y_lo: 4; y = y_hi * 4 + y_lo), z: 8, core: 2. Of those that a mesh axis runs over, the one named last changes fastest.
Arguments:
- data_rhs: float32 [32, 16, 64, 1536], P('subj', None, 'slab'), may hold values from -12 to 12
- inv_var: float32 [32, 64, 1536], P('subj', 'slab'), may hold values from 0.01 to 0.3
- design: float32 [32, 16], P('subj'), may hold values from 0.5 to 4
- keep_mask: int32 [32, 64, 1536], P('subj', 'slab'), may hold values 0 or 1
- brain_mask: int32 [64, 1536], P('slab'), may hold values 0 or 1
- tissue: int32 [64, 1536], P('slab'), may hold values from 0 to 2
- kappa_sq: float32 [3, 16], replicated, may hold values from 0.005 to 0.5
- prior_scale: float32 [16], replicated, may hold values from 0.5 to 2
- mean_field: float32 [16, 64, 1536], P(None, 'slab', 'subj'), may hold values from -6 to 6
- pop_noise: float32 [16, 64, 1536], P(None, 'slab', 'subj'), may hold values from -6 to 6
Outputs:
- subject_fields: float32 [32, 16, 64, 1536], P('subj', None, 'slab')
- new_mean: float32 [16, 64, 1536], P(None, 'slab', 'subj')
All inputs are finite; a program needn't handle non-finite values. No bound on the sum of `keep_mask` or of `brain_mask` on one device may be relied on, other than what follows from the above.
Results may differ from a plain program's by a relative error of at most 0.00016.
Values sent between devices are 32-bit elements; how exact they have to be, the bound alone decides.
A program may use at most 64 MiB of HBM per device.

v0:
```python
import math
import jax
import jax.numpy as jnp
from jax import lax
from jax.sharding import PartitionSpec as P

CLASSES = 3
ITERS = 8
CX = 64
MEAN_PRECISION = 1.0


def padded_2(cells, sides, width):
    for axis, dim in sides:
        count = lax.axis_size(axis)
        ends = count - 1
        head = lax.slice_in_dim(cells, 0, width, axis=dim)
        tail = lax.slice_in_dim(cells, cells.shape[dim] - width, cells.shape[dim], axis=dim)
        cells = jnp.concatenate(
            [
                lax.ppermute(tail, axis, [(i, (i + 1) % count) for i in range(ends)]),
                cells,
                lax.ppermute(head, axis, [((i + 1) % count, i) for i in range(ends)]),
            ],
            axis=dim,
        )
    return cells


def plane_beside(center):
    cells = center.shape[-1]
    column = lax.iota(jnp.int32, cells) % CX
    zeros_one = jnp.zeros(center.shape[:-1] + (1,), jnp.float32)
    zeros_row = jnp.zeros(center.shape[:-1] + (CX,), jnp.float32)
    from_left = jnp.where(column > 0, jnp.concatenate([zeros_one, center[..., :-1]], axis=-1), 0.0)
    from_right = jnp.where(
        column < CX - 1, jnp.concatenate([center[..., 1:], zeros_one], axis=-1), 0.0
    )
    from_below = jnp.concatenate([zeros_row, center[..., :-CX]], axis=-1)
    from_above = jnp.concatenate([center[..., CX:], zeros_row], axis=-1)
    return from_left + from_right + from_below + from_above


def beside_of(padded):
    center = padded[:, :, 1:-1]
    return padded[:, :, 2:] + padded[:, :, :-2] + plane_beside(center)


def local(
    data_rhs,
    inv_var,
    design,
    keep_mask,
    brain_mask,
    tissue,
    kappa_sq,
    prior_scale,
    mean_field,
    pop_noise,
):
    in_brain = brain_mask.astype(jnp.float32)
    kappa_field = jnp.zeros((prior_scale.shape[0],) + tissue.shape, jnp.float32)
    for label in range(CLASSES):
        kappa_field = (
            kappa_field
            + jnp.where(tissue == label, 1.0, 0.0)[None] * kappa_sq[label][:, None, None]
        )
    scale_col = prior_scale[:, None, None]
    shifted = 6.0 + kappa_field
    whole_mean = lax.all_gather(mean_field, "subj", axis=2, tiled=True)
    padded_mean = padded_2(whole_mean[None], (("slab", 2),), 1)
    prior_mean = scale_col * (shifted * padded_mean[:, :, 1:-1] - beside_of(padded_mean))
    voxel_factor = inv_var * in_brain * keep_mask.astype(jnp.float32)
    diagonal = design[:, :, None, None] * voxel_factor[:, None] + scale_col * shifted
    right_side = data_rhs + prior_mean

    def inner(left, right):
        return jnp.sum(left * right, axis=(2, 3))

    solution = jnp.zeros_like(right_side)
    residual = right_side

    def residual_norm(current):
        local_norm = inner(current, current)
        return lax.psum(local_norm, "slab")

    direction = right_side
    norm_now = residual_norm(residual)
    for iteration in range(ITERS):
        applied = diagonal * direction - scale_col * beside_of(
            padded_2(direction, (("slab", 2),), 1)
        )
        local_curv = inner(direction, applied)
        curv_sum = lax.psum(local_curv, "slab")
        step_size = norm_now / curv_sum
        solution = solution + step_size[:, :, None, None] * direction
        if iteration + 1 < ITERS:
            residual = residual - step_size[:, :, None, None] * applied
            norm_next = residual_norm(residual)
            direction = residual + (norm_next / norm_now)[:, :, None, None] * direction
            norm_now = norm_next
    subject_total = jnp.sum(solution, axis=0)
    summed = lax.psum_scatter(subject_total, "subj", scatter_dimension=2, tiled=True)
    subjects = design.shape[0] * lax.axis_size("subj")
    divisor = subjects + MEAN_PRECISION
    new_mean = summed / divisor + pop_noise / math.sqrt(divisor)
    return (solution, new_mean)


def solution(mesh):
    in_specs = (
        P("subj", None, "slab", None),
        P("subj", "slab", None),
        P("subj", None),
        P("subj", "slab", None),
        P("slab", None),
        P("slab", None),
        P(),
        P(),
        P(None, "slab", "subj"),
        P(None, "slab", "subj"),
    )
    out_specs = (P("subj", None, "slab", None), P(None, "slab", "subj"))
    return jax.shard_map(local, mesh=mesh, in_specs=in_specs, out_specs=out_specs, check_vma=False)
```

profile of v0, /device:TPU:4, one launch (start us, length us, event | category | flops | bytes accessed | tf_op | source)
XLA Modules:
  0.0 1116.8 jit_solution(7056748842792953106)
XLA Ops:
  8.1 126.5 %all_gather.3 = f32[16,4,1536]{0,1,2:T(4,128)} all-gather(f32[16,4,48]{0,1,2:T(4,128)S(1)} %copy.79), channel_id=1, replica_groups=mesh['subj'=32,'slab'=16] {'subj'}, dimensions={2}, use_global_device_ids=true | all-gather | bytes 405504 | tf_op jit(solution)/shard_map/all_gather | solution.py:70
  134.6 3.1 copy.80
  137.7 1.9 collective-permute-start
  139.6 2.4 collective-permute-start.1
  147.2 2.4 collective-permute-start.2
  149.6 1.9 collective-permute-start.3
  151.8 3.7 collective-permute-done.3
  156.1 40.7 %all-reduce.36 = (f32[1,16]{1,0:T(1,128)S(1)}, f32[1,16]{1,0:T(1,128)S(1)}) all-reduce(f32[1,16]{1,0:T(1,128)S(1)} %bitcast.85, f32[1,16]{1,0:T(1,128)S(1)} %bitcast.84), channel_id=1, replica_groups=mesh['subj'=32,'slab'=16] {'slab'}, use_global_device_ids=true, to_apply=%region_1.2 | all-reduce | flops 32 | bytes 256 | tf_op jit(solution)/shard_map/psum | solution.py:85
  197.0 42.8 %psum.114 = f32[1,16]{1,0:T(1,128)S(1)} all-reduce(f32[1,16]{1,0:T(1,128)S(1)} %bitcast.90), channel_id=1, replica_groups=mesh['subj'=32,'slab'=16] {'slab'}, use_global_device_ids=true, to_apply=%region_5.6 | all-reduce | flops 16 | bytes 128 | tf_op jit(solution)/shard_map/psum | solution.py:85
  240.3 1.9 collective-permute-start.4
  242.2 2.5 collective-permute-start.5
  244.9 3.3 collective-permute-done.5
  249.3 48.8 %psum.115 = f32[1,16]{1,0:T(1,128)S(1)} all-reduce(f32[1,16]{1,0:T(1,128)S(1)} %bitcast.92), channel_id=1, replica_groups=mesh['subj'=32,'slab'=16] {'slab'}, use_global_device_ids=true, to_apply=%region_7.8 | all-reduce | flops 16 | bytes 128 | tf_op jit(solution)/shard_map/psum | solution.py:94
  299.7 42.8 %psum.116 = f32[1,16]{1,0:T(1,128)S(1)} all-reduce(f32[1,16]{1,0:T(1,128)S(1)} %bitcast.82), channel_id=1, replica_groups=mesh['subj'=32,'slab'=16] {'slab'}, use_global_device_ids=true, to_apply=%region_9.10 | all-reduce | flops 16 | bytes 128 | tf_op jit(solution)/shard_map/psum | solution.py:85
  343.4 1.9 collective-permute-start.6
  345.4 2.5 collective-permute-start.7
  348.0 3.3 collective-permute-done.7
  352.5 48.8 %psum.117 = f32[1,16]{1,0:T(1,128)S(1)} all-reduce(f32[1,16]{1,0:T(1,128)S(1)} %bitcast.93), channel_id=1, replica_groups=mesh['subj'=32,'slab'=16] {'slab'}, use_global_device_ids=true, to_apply=%region_11.12 | all-reduce | flops 16 | bytes 128 | tf_op jit(solution)/shard_map/psum | solution.py:94
  402.2 42.8 %psum.118 = f32[1,16]{1,0:T(1,128)S(1)} all-reduce(f32[1,16]{1,0:T(1,128)S(1)} %bitcast.86), channel_id=1, replica_groups=mesh['subj'=32,'slab'=16] {'slab'}, use_global_device_ids=true, to_apply=%region_13.14 | all-reduce | flops 16 | bytes 128 | tf_op jit(solution)/shard_map/psum | solution.py:85
  446.0 1.9 collective-permute-start.8
  447.9 2.5 collective-permute-start.9
  450.6 3.3 collective-permute-done.9
  455.0 48.8 %psum.119 = f32[1,16]{1,0:T(1,128)S(1)} all-reduce(f32[1,16]{1,0:T(1,128)S(1)} %bitcast.94), channel_id=1, replica_groups=mesh['subj'=32,'slab'=16] {'slab'}, use_global_device_ids=true, to_apply=%region_15.16 | all-reduce | flops 16 | bytes 128 | tf_op jit(solution)/shard_map/psum | solution.py:94
  504.7 42.8 %psum.120 = f32[1,16]{1,0:T(1,128)S(1)} all-reduce(f32[1,16]{1,0:T(1,128)S(1)} %bitcast.87), channel_id=1, replica_groups=mesh['subj'=32,'slab'=16] {'slab'}, use_global_device_ids=true, to_apply=%region_17.18 | all-reduce | flops 16 | bytes 128 | tf_op jit(solution)/shard_map/psum | solution.py:85
  548.5 1.9 collective-permute-start.10
  550.4 2.5 collective-permute-start.11
  553.1 3.3 collective-permute-done.11
  557.5 48.8 %psum.121 = f32[1,16]{1,0:T(1,128)S(1)} all-reduce(f32[1,16]{1,0:T(1,128)S(1)} %bitcast.95), channel_id=1, replica_groups=mesh['subj'=32,'slab'=16] {'slab'}, use_global_device_ids=true, to_apply=%region_19.20 | all-reduce | flops 16 | bytes 128 | tf_op jit(solution)/shard_map/psum | solution.py:94
  607.3 42.8 %psum.122 = f32[1,16]{1,0:T(1,128)S(1)} all-reduce(f32[1,16]{1,0:T(1,128)S(1)} %bitcast.88), channel_id=1, replica_groups=mesh['subj'=32,'slab'=16] {'slab'}, use_global_device_ids=true, to_apply=%region_21.22 | all-reduce | flops 16 | bytes 128 | tf_op jit(solution)/shard_map/psum | solution.py:85
  651.0 1.9 collective-permute-start.12
  653.0 2.5 collective-permute-start.13
  655.6 3.3 collective-permute-done.13
  660.1 48.8 %psum.123 = f32[1,16]{1,0:T(1,128)S(1)} all-reduce(f32[1,16]{1,0:T(1,128)S(1)} %bitcast.96), channel_id=1, replica_groups=mesh['subj'=32,'slab'=16] {'slab'}, use_global_device_ids=true, to_apply=%region_23.24 | all-reduce | flops 16 | bytes 128 | tf_op jit(solution)/shard_map/psum | solution.py:94
  710.4 42.9 %psum.124 = f32[1,16]{1,0:T(1,128)S(1)} all-reduce(f32[1,16]{1,0:T(1,128)} %bitcast.89), channel_id=1, replica_groups=mesh['subj'=32,'slab'=16] {'slab'}, use_global_device_ids=true, to_apply=%region_25.26 | all-reduce | flops 16 | bytes 128 | tf_op jit(solution)/shard_map/psum | solution.py:85
  754.2 1.9 collective-permute-start.14
  756.2 2.5 collective-permute-start.15
  758.8 3.3 collective-permute-done.15
  762.1 1.8 multiply_reduce_fusion.1
  764.0 49.5 %psum.125 = f32[1,16]{1,0:T(1,128)} all-reduce(f32[1,16]{1,0:T(1,128)} %bitcast.97), channel_id=1, replica_groups=mesh['subj'=32,'slab'=16] {'slab'}, use_global_device_ids=true, to_apply=%region_27.28 | all-reduce | flops 16 | bytes 128 | tf_op jit(solution)/shard_map/psum | solution.py:94
  815.4 43.4 %psum.126 = f32[1,16]{1,0:T(1,128)} all-reduce(f32[1,16]{1,0:T(1,128)} %bitcast.91), channel_id=1, replica_groups=mesh['subj'=32,'slab'=16] {'slab'}, use_global_device_ids=true, to_apply=%region_29.30 | all-reduce | flops 16 | bytes 128 | tf_op jit(solution)/shard_map/psum | solution.py:85
  860.8 1.9 collective-permute-start.16
  862.7 2.5 collective-permute-start.17
  865.4 3.3 collective-permute-done.17
  868.7 1.8 fusion.5
  870.5 49.1 %psum.127 = f32[1,16]{1,0:T(1,128)S(1)} all-reduce(f32[1,16]{1,0:T(1,128)} %bitcast.83), channel_id=1, replica_groups=mesh['subj'=32,'slab'=16] {'slab'}, use_global_device_ids=true, to_apply=%region_31.32 | all-reduce | flops 16 | bytes 128 | tf_op jit(solution)/shard_map/psum | solution.py:94
  921.3 8.3 copy.85
  929.6 9.8 reshape.112
  940.5 167.6 %reduce-scatter.4.cloned.1.call-done = f32[48,64]{1,0:T(8,128)} async-done(((f32[1536,64]{1,0:T(8,128)}), f32[48,64]{1,0:T(8,128)}) %reduce-scatter.4.cloned.1.call-update) | async-done | bytes 12304
  (129 shorter events, 33.6 us)
Async XLA Ops:
  7.2 148.4 %copy-start.6 = (f32[16]{0:T(128)S(1)}, f32[16]{0:T(128)}, u32[]{:S(2)}) copy-start(f32[16]{0:T(128)} %param.17) | copy-start | bytes 196
  7.2 148.4 %copy-start.8 = (f32[1,16]{1,0:T(1,128)S(1)}, f32[1,16]{1,0:T(1,128)}, u32[]{:S(2)}) copy-start(f32[1,16]{1,0:T(1,128)} %param.12) | copy-start | bytes 196
  7.2 1100.9 %reduce-scatter.4.cloned.1.call-start = ((), (), s32[]{:S(2)}) async-start(), calls=%async_computation.1 | async-start | bytes 811008
  137.7 7.1 collective-permute-start
  139.6 5.9 collective-permute-start.1
  143.2 96.9 %copy-start.5 = (f32[16]{0:T(128)}, f32[16]{0:T(128)S(1)}, u32[]{:S(2)}) copy-start(f32[16]{0:T(128)S(1)} %get-tuple-element.94) | copy-start | bytes 196
  144.0 514.9 %copy-start.1 = (f32[4,1536]{1,0:T(4,128)}, f32[4,1536]{1,0:T(4,128)S(1)}, u32[]{:S(2)}) copy-start(f32[4,1536]{1,0:T(4,128)S(1)} %get-tuple-element.89) | copy-start | bytes 73732
  144.0 514.9 %copy-start.2 = (f32[4,1536]{1,0:T(4,128)}, f32[4,1536]{1,0:T(4,128)S(1)}, u32[]{:S(2)}) copy-start(f32[4,1536]{1,0:T(4,128)S(1)} %get-tuple-element.90) | copy-start | bytes 73732
  144.0 514.9 %copy-start.3 = (f32[4,1536]{1,0:T(4,128)}, f32[4,1536]{1,0:T(4,128)S(1)}, u32[]{:S(2)}) copy-start(f32[4,1536]{1,0:T(4,128)S(1)} %get-tuple-element.91) | copy-start | bytes 73732
  144.8 514.1 %copy-start.4 = (f32[4,1536]{1,0:T(4,128)}, f32[4,1536]{1,0:T(4,128)S(1)}, u32[]{:S(2)}) copy-start(f32[4,1536]{1,0:T(4,128)S(1)} %fusion.40) | copy-start | bytes 73732
  147.2 4.6 collective-permute-start.2
  149.6 5.9 collective-permute-start.3
  196.7 43.4 %copy-start.9 = (f32[16]{0:T(128)}, f32[16]{0:T(128)S(1)}, u32[]{:S(2)}) copy-start(f32[16]{0:T(128)S(1)} %divide_bitcast_fusion.14) | copy-start | bytes 196
  239.8 0.5 copy-start.20
  240.3 4.6 collective-permute-start.4
  242.2 5.9 collective-permute-start.5
  298.8 44.6 %copy-start.11 = (f32[16]{0:T(128)}, f32[16]{0:T(128)S(1)}, u32[]{:S(2)}) copy-start(f32[16]{0:T(128)S(1)} %divide_bitcast_fusion.12) | copy-start | bytes 196
  342.4 1.0 copy-start.16
  343.4 4.6 collective-permute-start.6
  345.4 5.9 collective-permute-start.7
  401.9 44.0 %copy-start.12 = (f32[16]{0:T(128)}, f32[16]{0:T(128)S(1)}, u32[]{:S(2)}) copy-start(f32[16]{0:T(128)S(1)} %divide_bitcast_fusion.10) | copy-start | bytes 196
  445.0 1.0 copy-start.17
  446.0 4.6 collective-permute-start.8
  447.9 5.9 collective-permute-start.9
  504.5 44.0 %copy-start.13 = (f32[16]{0:T(128)}, f32[16]{0:T(128)S(1)}, u32[]{:S(2)}) copy-start(f32[16]{0:T(128)S(1)} %divide_bitcast_fusion.8) | copy-start | bytes 196
  547.5 1.0 copy-start.18
  548.5 4.6 collective-permute-start.10
  550.4 5.9 collective-permute-start.11
  607.0 51.9 %copy-start.14 = (f32[16]{0:T(128)}, f32[16]{0:T(128)S(1)}, u32[]{:S(2)}) copy-start(f32[16]{0:T(128)S(1)} %divide_bitcast_fusion.6) | copy-start | bytes 196
  650.0 8.9 copy-start.19
  651.0 4.6 collective-permute-start.12
  653.0 5.9 collective-permute-start.13
  709.6 0.8 copy-start.15
  753.3 0.7 copy-start.21
  754.2 4.6 collective-permute-start.14
  756.2 5.9 collective-permute-start.15
  763.9 94.9 %copy-start = (f32[1,16,4,1536]{3,1,2,0:T(8,128)}, f32[1,16,4,1536]{3,1,2,0:T(8,128)S(1)}, u32[]{:S(2)}) copy-start(f32[1,16,4,1536]{3,1,2,0:T(8,128)S(1)} %get-tuple-element.13) | copy-start | bytes 1179652
  814.0 0.5 copy-start.10
  860.8 4.6 collective-permute-start.16
  862.7 5.9 collective-permute-start.17
  921.3 188.0 %copy-start.7 = (f32[16,4,48]{2,1,0:T(4,128)S(1)}, f32[16,4,48]{2,1,0:T(4,128)}, u32[]{:S(2)}) copy-start(f32[16,4,48]{2,1,0:T(4,128)} %param.19) | copy-start | bytes 36868
Sparse Core Ops, SparseCore 0:
  939.6 168.4 reduce-scatter.3
where the time goes:
time: 1120 us
  blocking collectives  810 us (72%)
  waiting for transfers between devices  195 us (17%)
  starting transfers between devices  39.5 us (4%)
  local copies, waits for them, and re-layouts  29 us (3%)
  other arithmetic  28.6 us (3%)
  between operations  14.6 us (1%)
    psum x7, blocking collectives, local(): curv_sum = lax.psum(local_curv, 'slab')  343 us
    psum x8, blocking collectives, residual_norm(): return lax.psum(local_norm, 'slab')  341 us
    unnamed x2, waiting for transfers between devices  168 us
    all_gather x1, blocking collectives, local(): whole_mean = lax.all_gather(mean_field, 'subj', axis=2, tiled=True)  127 us
    ppermute x9, waiting for transfers between devices, padded_2(): lax.ppermute(tail, axis, [(i, (i + 1) % count) for i in range(ends)])  27.4 us
  transfers between devices with their start and end apart: 19, of which 11 were waited for; matrix products, arithmetic and copies ran while one was open for 0% of the time, Pallas kernels for 0%

commit v1 on v0

--- a/solution.py
+++ b/solution.py
@@ -67,7 +67,12 @@
         )
     scale_col = prior_scale[:, None, None]
     shifted = 6.0 + kappa_field
-    whole_mean = lax.all_gather(mean_field, "subj", axis=2, tiled=True)
+    whole_mean = jnp.concatenate(
+        lax.all_to_all(
+            jnp.stack([mean_field for _ in range(lax.axis_size("subj"))], 0), "subj", 0, 0
+        ),
+        2,
+    )
     padded_mean = padded_2(whole_mean[None], (("slab", 2),), 1)
     prior_mean = scale_col * (shifted * padded_mean[:, :, 1:-1] - beside_of(padded_mean))
     voxel_factor = inv_var * in_brain * keep_mask.astype(jnp.float32)

time: 1120 us -> 1030 us (0.920)
  the two profiles are of different devices: /device:TPU:4 before, /device:TPU:6 now
where the time goes in v1:
time: 1030 us
  blocking collectives  694 us (67%)
  waiting for transfers between devices  202 us (20%)
  starting transfers between devices  56.3 us (5%)
  local copies, waits for them, and re-layouts  31 us (3%)
  other arithmetic  29.1 us (3%)
  between operations  14.6 us (1%)
    psum x8, blocking collectives, residual_norm(): return lax.psum(local_norm, 'slab')  352 us
    psum x7, blocking collectives, local(): curv_sum = lax.psum(local_curv, 'slab')  342 us
    unnamed x2, waiting for transfers between devices  163 us
    ppermute x9, waiting for transfers between devices, padded_2(): lax.ppermute(tail, axis, [(i, (i + 1) % count) for i in range(ends)])  26.8 us
    ppermute x9, starting transfers between devices, padded_2(): lax.ppermute(tail, axis, [(i, (i + 1) % count) for i in range(ends)])  25.2 us
    unnamed x53, local copies, waits for them, and re-layouts  24.2 us
  transfers between devices with their start and end apart: 20, of which 11 were waited for; matrix products, arithmetic and copies ran while one was open for 0% of the time, Pallas kernels for 0%

profile of v1, /device:TPU:6, one launch (start us, length us, event | category | flops | bytes accessed | tf_op | source)
XLA Modules:
  0.0 1027.6 jit_solution(11373890814411751842)
XLA Ops:
  8.2 1.9 reshape.131
  10.2 13.7 %all-to-all-start = ((f32[32,1,3072]{2,1,0:T(1,128)}), f32[32,1,3072]{2,1,0:T(1,128)S(1)}, u32[]{:S(2)}, u32[]{:S(2)}) async-start(f32[32,1,3072]{2,1,0:T(1,128)} %reshape.131), calls=%async_computation | async-start | bytes 786432 | tf_op jit(solution)/shard_map/all_to_all | solution.py:71
  26.4 12.4 %all-to-all-done = f32[32,1,3072]{2,1,0:T(1,128)S(1)} async-done(((f32[32,1,3072]{2,1,0:T(1,128)}), f32[32,1,3072]{2,1,0:T(1,128)S(1)}, u32[]{:S(2)}, u32[]{:S(2)}) %all-to-all-start) | async-done | bytes 393248 | tf_op jit(solution)/shard_map/all_to_all | solution.py:71
  43.4 1.9 collective-permute-start
  45.4 2.4 collective-permute-start.1
  48.0 3.3 collective-permute-done.1
  51.9 1.9 collective-permute-start.2
  53.8 5.2 collective-permute-start.3
  60.5 51.6 %all-reduce.36 = (f32[1,16]{1,0:T(1,128)S(1)}, f32[1,16]{1,0:T(1,128)S(1)}) all-reduce(f32[1,16]{1,0:T(1,128)S(1)} %bitcast.84, f32[1,16]{1,0:T(1,128)S(1)} %bitcast.83), channel_id=1, replica_groups=mesh['subj'=32,'slab'=16] {'slab'}, use_global_device_ids=true, to_apply=%region_1.2 | all-reduce | flops 32 | bytes 256 | tf_op jit(solution)/shard_map/psum | solution.py:90
  112.4 42.8 %psum.114 = f32[1,16]{1,0:T(1,128)S(1)} all-reduce(f32[1,16]{1,0:T(1,128)S(1)} %bitcast.89), channel_id=1, replica_groups=mesh['subj'=32,'slab'=16] {'slab'}, use_global_device_ids=true, to_apply=%region_5.6 | all-reduce | flops 16 | bytes 128 | tf_op jit(solution)/shard_map/psum | solution.py:90
  155.7 1.9 collective-permute-start.4
  157.6 2.5 collective-permute-start.5
  160.2 3.3 collective-permute-done.5
  164.7 48.8 %psum.115 = f32[1,16]{1,0:T(1,128)S(1)} all-reduce(f32[1,16]{1,0:T(1,128)S(1)} %bitcast.91), channel_id=1, replica_groups=mesh['subj'=32,'slab'=16] {'slab'}, use_global_device_ids=true, to_apply=%region_7.8 | all-reduce | flops 16 | bytes 128 | tf_op jit(solution)/shard_map/psum | solution.py:99
  215.0 42.8 %psum.116 = f32[1,16]{1,0:T(1,128)S(1)} all-reduce(f32[1,16]{1,0:T(1,128)S(1)} %bitcast.81), channel_id=1, replica_groups=mesh['subj'=32,'slab'=16] {'slab'}, use_global_device_ids=true, to_apply=%region_9.10 | all-reduce | flops 16 | bytes 128 | tf_op jit(solution)/shard_map/psum | solution.py:90
  258.8 1.9 collective-permute-start.6
  260.7 2.5 collective-permute-start.7
  263.4 3.3 collective-permute-done.7
  267.8 48.8 %psum.117 = f32[1,16]{1,0:T(1,128)S(1)} all-reduce(f32[1,16]{1,0:T(1,128)S(1)} %bitcast.92), channel_id=1, replica_groups=mesh['subj'=32,'slab'=16] {'slab'}, use_global_device_ids=true, to_apply=%region_11.12 | all-reduce | flops 16 | bytes 128 | tf_op jit(solution)/shard_map/psum | solution.py:99
  317.5 42.8 %psum.118 = f32[1,16]{1,0:T(1,128)S(1)} all-reduce(f32[1,16]{1,0:T(1,128)S(1)} %bitcast.85), channel_id=1, replica_groups=mesh['subj'=32,'slab'=16] {'slab'}, use_global_device_ids=true, to_apply=%region_13.14 | all-reduce | flops 16 | bytes 128 | tf_op jit(solution)/shard_map/psum | solution.py:90
  361.3 1.9 collective-permute-start.8
  363.2 2.5 collective-permute-start.9
  365.9 3.3 collective-permute-done.9
  370.3 48.8 %psum.119 = f32[1,16]{1,0:T(1,128)S(1)} all-reduce(f32[1,16]{1,0:T(1,128)S(1)} %bitcast.93), channel_id=1, replica_groups=mesh['subj'=32,'slab'=16] {'slab'}, use_global_device_ids=true, to_apply=%region_15.16 | all-reduce | flops 16 | bytes 128 | tf_op jit(solution)/shard_map/psum | solution.py:99
  420.0 42.8 %psum.120 = f32[1,16]{1,0:T(1,128)S(1)} all-reduce(f32[1,16]{1,0:T(1,128)S(1)} %bitcast.86), channel_id=1, replica_groups=mesh['subj'=32,'slab'=16] {'slab'}, use_global_device_ids=true, to_apply=%region_17.18 | all-reduce | flops 16 | bytes 128 | tf_op jit(solution)/shard_map/psum | solution.py:90
  463.8 1.9 collective-permute-start.10
  465.7 2.7 collective-permute-start.11
  468.6 3.1 collective-permute-done.11
  472.9 48.8 %psum.121 = f32[1,16]{1,0:T(1,128)S(1)} all-reduce(f32[1,16]{1,0:T(1,128)S(1)} %bitcast.94), channel_id=1, replica_groups=mesh['subj'=32,'slab'=16] {'slab'}, use_global_device_ids=true, to_apply=%region_19.20 | all-reduce | flops 16 | bytes 128 | tf_op jit(solution)/shard_map/psum | solution.py:99
  522.6 42.8 %psum.122 = f32[1,16]{1,0:T(1,128)S(1)} all-reduce(f32[1,16]{1,0:T(1,128)S(1)} %bitcast.87), channel_id=1, replica_groups=mesh['subj'=32,'slab'=16] {'slab'}, use_global_device_ids=true, to_apply=%region_21.22 | all-reduce | flops 16 | bytes 128 | tf_op jit(solution)/shard_map/psum | solution.py:90
  566.4 1.9 collective-permute-start.12
  568.3 2.5 collective-permute-start.13
  571.0 3.3 collective-permute-done.13
  575.4 48.8 %psum.123 = f32[1,16]{1,0:T(1,128)S(1)} all-reduce(f32[1,16]{1,0:T(1,128)S(1)} %bitcast.95), channel_id=1, replica_groups=mesh['subj'=32,'slab'=16] {'slab'}, use_global_device_ids=true, to_apply=%region_23.24 | all-reduce | flops 16 | bytes 128 | tf_op jit(solution)/shard_map/psum | solution.py:99
  625.7 42.9 %psum.124 = f32[1,16]{1,0:T(1,128)S(1)} all-reduce(f32[1,16]{1,0:T(1,128)} %bitcast.88), channel_id=1, replica_groups=mesh['subj'=32,'slab'=16] {'slab'}, use_global_device_ids=true, to_apply=%region_25.26 | all-reduce | flops 16 | bytes 128 | tf_op jit(solution)/shard_map/psum | solution.py:90
  669.6 1.9 collective-permute-start.14
  671.5 2.5 collective-permute-start.15
  674.2 3.3 collective-permute-done.15
  677.4 1.8 multiply_reduce_fusion.1
  679.3 49.4 %psum.125 = f32[1,16]{1,0:T(1,128)} all-reduce(f32[1,16]{1,0:T(1,128)} %bitcast.96), channel_id=1, replica_groups=mesh['subj'=32,'slab'=16] {'slab'}, use_global_device_ids=true, to_apply=%region_27.28 | all-reduce | flops 16 | bytes 128 | tf_op jit(solution)/shard_map/psum | solution.py:99
  730.7 43.4 %psum.126 = f32[1,16]{1,0:T(1,128)} all-reduce(f32[1,16]{1,0:T(1,128)} %bitcast.90), channel_id=1, replica_groups=mesh['subj'=32,'slab'=16] {'slab'}, use_global_device_ids=true, to_apply=%region_29.30 | all-reduce | flops 16 | bytes 128 | tf_op jit(solution)/shard_map/psum | solution.py:90
  776.1 1.9 collective-permute-start.16
  778.0 2.5 collective-permute-start.17
  780.7 3.3 collective-permute-done.17
  785.8 48.9 %psum.127 = f32[1,16]{1,0:T(1,128)S(1)} all-reduce(f32[1,16]{1,0:T(1,128)} %bitcast.82), channel_id=1, replica_groups=mesh['subj'=32,'slab'=16] {'slab'}, use_global_device_ids=true, to_apply=%region_31.32 | all-reduce | flops 16 | bytes 128 | tf_op jit(solution)/shard_map/psum | solution.py:99
  836.4 8.3 copy.16
  844.7 9.8 reshape.129
  855.6 163.3 %reduce-scatter.4.cloned.1.call-done = f32[48,64]{1,0:T(8,128)} async-done(((f32[1536,64]{1,0:T(8,128)}), f32[48,64]{1,0:T(8,128)}) %reduce-scatter.4.cloned.1.call-update) | async-done | bytes 12304
  (137 shorter events, 39.0 us)
Async XLA Ops:
  7.2 44.2 %copy-start.7 = (f32[16]{0:T(128)S(1)}, f32[16]{0:T(128)}, u32[]{:S(2)}) copy-start(f32[16]{0:T(128)} %param.17) | copy-start | bytes 196
  7.2 44.1 %copy-start.5 = (f32[1,16,4,1536]{3,2,1,0:T(4,128)S(1)}, f32[1,16,4,1536]{3,2,1,0:T(4,128)}, u32[]{:S(2)}) copy-start(f32[1,16,4,1536]{3,2,1,0:T(4,128)} %param.10) | copy-start | bytes 1179652
  7.2 52.8 %copy-start.9 = (f32[1,16]{1,0:T(1,128)S(1)}, f32[1,16]{1,0:T(1,128)}, u32[]{:S(2)}) copy-start(f32[1,16]{1,0:T(1,128)} %param.12) | copy-start | bytes 196
  10.2 28.6 %all-to-all-start = ((f32[32,1,3072]{2,1,0:T(1,128)}), f32[32,1,3072]{2,1,0:T(1,128)S(1)}, u32[]{:S(2)}, u32[]{:S(2)}) async-start(f32[32,1,3072]{2,1,0:T(1,128)} %reshape.131), calls=%async_computation | async-start | bytes 786432 | tf_op jit(solution)/shard_map/all_to_all | solution.py:71
  23.9 995.0 %reduce-scatter.4.cloned.1.call-start = ((), (), s32[]{:S(2)}) async-start(), calls=%async_computation.2 | async-start | bytes 811008
  24.7 549.5 %copy-start.1 = (f32[4,1536]{1,0:T(4,128)}, f32[4,1536]{1,0:T(4,128)S(1)}, u32[]{:S(2)}) copy-start(f32[4,1536]{1,0:T(4,128)S(1)} %get-tuple-element.85) | copy-start | bytes 73732
  24.7 549.5 %copy-start.3 = (f32[4,1536]{1,0:T(4,128)}, f32[4,1536]{1,0:T(4,128)S(1)}, u32[]{:S(2)}) copy-start(f32[4,1536]{1,0:T(4,128)S(1)} %get-tuple-element.87) | copy-start | bytes 73732
  24.7 600.2 %copy-start.2 = (f32[4,1536]{1,0:T(4,128)}, f32[4,1536]{1,0:T(4,128)S(1)}, u32[]{:S(2)}) copy-start(f32[4,1536]{1,0:T(4,128)S(1)} %get-tuple-element.86) | copy-start | bytes 73732
  25.6 129.9 %copy-start.6 = (f32[16]{0:T(128)}, f32[16]{0:T(128)S(1)}, u32[]{:S(2)}) copy-start(f32[16]{0:T(128)S(1)} %get-tuple-element.90) | copy-start | bytes 196
  26.4 547.9 %copy-start.4 = (f32[4,1536]{1,0:T(4,128)}, f32[4,1536]{1,0:T(4,128)S(1)}, u32[]{:S(2)}) copy-start(f32[4,1536]{1,0:T(4,128)S(1)} %fusion.40) | copy-start | bytes 73732
  43.4 4.5 collective-permute-start
  45.4 5.9 collective-permute-start.1
  51.9 7.4 collective-permute-start.2
  53.8 6.2 collective-permute-start.3
  112.1 43.4 %copy-start.10 = (f32[16]{0:T(128)}, f32[16]{0:T(128)S(1)}, u32[]{:S(2)}) copy-start(f32[16]{0:T(128)S(1)} %divide_bitcast_fusion.14) | copy-start | bytes 196
  155.2 0.5 copy-start.21
  155.7 4.6 collective-permute-start.4
  157.6 5.9 collective-permute-start.5
  214.1 44.6 %copy-start.12 = (f32[16]{0:T(128)}, f32[16]{0:T(128)S(1)}, u32[]{:S(2)}) copy-start(f32[16]{0:T(128)S(1)} %divide_bitcast_fusion.12) | copy-start | bytes 196
  257.8 1.0 copy-start.17
  258.8 4.6 collective-permute-start.6
  260.7 5.9 collective-permute-start.7
  317.3 44.0 %copy-start.13 = (f32[16]{0:T(128)}, f32[16]{0:T(128)S(1)}, u32[]{:S(2)}) copy-start(f32[16]{0:T(128)S(1)} %divide_bitcast_fusion.10) | copy-start | bytes 196
  360.3 1.0 copy-start.18
  361.3 4.6 collective-permute-start.8
  363.2 5.9 collective-permute-start.9
  419.8 44.0 %copy-start.14 = (f32[16]{0:T(128)}, f32[16]{0:T(128)S(1)}, u32[]{:S(2)}) copy-start(f32[16]{0:T(128)S(1)} %divide_bitcast_fusion.8) | copy-start | bytes 196
  462.8 1.0 copy-start.19
  463.8 4.8 collective-permute-start.10
  465.7 5.9 collective-permute-start.11
  522.3 51.9 %copy-start.15 = (f32[16]{0:T(128)}, f32[16]{0:T(128)S(1)}, u32[]{:S(2)}) copy-start(f32[16]{0:T(128)S(1)} %divide_bitcast_fusion.6) | copy-start | bytes 196
  565.4 8.9 copy-start.20
  566.4 4.6 collective-permute-start.12
  568.3 5.9 collective-permute-start.13
  624.9 0.8 copy-start.16
  668.6 0.7 copy-start.22
  669.6 4.6 collective-permute-start.14
  671.5 5.9 collective-permute-start.15
  679.3 94.9 %copy-start = (f32[1,16,4,1536]{3,1,2,0:T(8,128)}, f32[1,16,4,1536]{3,1,2,0:T(8,128)S(1)}, u32[]{:S(2)}) copy-start(f32[1,16,4,1536]{3,1,2,0:T(8,128)S(1)} %get-tuple-element.9) | copy-start | bytes 1179652
  729.4 0.5 copy-start.11
  776.1 4.6 collective-permute-start.16
  778.0 5.9 collective-permute-start.17
  836.4 183.7 %copy-start.8 = (f32[16,4,48]{2,1,0:T(4,128)S(1)}, f32[16,4,48]{2,1,0:T(4,128)}, u32[]{:S(2)}) copy-start(f32[16,4,48]{2,1,0:T(4,128)} %param.19) | copy-start | bytes 36868
Sparse Core Ops, SparseCore 0:
  854.7 164.1 reduce-scatter.3
